TPU v7x, 128 devices: a whole 4x4x4 slice. The times are simulated.
128 devices in a mesh: grp: 8 (over z_lo, x), blk: 16 (over z_hi, y, core).
Axes of the slice: x: 4, y: 4, z: 4 (z_hi: 2, z_lo: 2; z = z_hi * 2 + z_lo), core: 2. Of those that a mesh axis runs over, the one named last changes fastest.
Arguments:
- feats: bfloat16 [131072, 256], P(('grp', 'blk')), may hold values from -6 to 6
- weight: bfloat16 [256, 256], replicated, may hold values from -0.375 to 0.375
- cotangent: bfloat16 [131072, 256], P(('grp', 'blk')), may hold values from -6 to 6
- labels: int32 [131072], P(('grp', 'blk')), may hold values from -86 to 171
- tile_vals: bfloat16 [8, 16, 16, 32, 128, 128], P('grp', 'blk'), may hold values from -0.0625 to 0.0625
- tile_row: int32 [8, 16, 16, 32], P('grp', 'blk'), may hold values from 0 to 7
- tile_col: int32 [8, 16, 16, 32], P('grp', 'blk'), may hold values from 0 to 7
- tile_count: int32 [8, 16, 16], P('grp', 'blk'), may hold values from 1 to 32, as said below
- hub_vals: bfloat16 [8, 16, 16, 128, 128], P('grp', 'blk'), may hold values from -0.0625 to 0.0625
- hub_col: int32 [8, 16, 16], P('grp', 'blk'), may hold values from 0 to 7
- hub_dest: int32 [8, 16, 16, 1], P(None, 'blk'), may hold values from 0 to 7; in each aligned block of 16 rows (0 to 15, 16 to 31, ..., all dimensions but the last counted through in order) at most 4 rows name the same one
- hub_row: int32 [8, 16, 16], P(None, 'blk'), may hold values from 0 to 7
Outputs:
- layer_out: bfloat16 [131072, 256], P(('grp', 'blk'))
- grad_feats: bfloat16 [131072, 256], P(('grp', 'blk'))
- grad_weight: float32 [256, 256], replicated
Inputs may be any that keep to these rules, and one draw needn't show every extreme that they name: Only the first tile_count slots of a device's list for a source block are used; some device uses all 32. `hub_dest`: at most 4 of the 16 hub tiles of one device name the same group, and exactly 4 in some devices.
All inputs are finite; a program needn't handle non-finite values.
Results may differ from a plain program's by a relative error of at most 0.007.
Values may be sent and summed in bfloat16 or wider, within the bound.
A program may use at most 192 MiB of HBM per device.

v0:
```python
import math
import jax
import jax.numpy as jnp
from jax import lax
from jax.sharding import PartitionSpec as P


def shifted(value, axis, by):
    size = lax.axis_size(axis)
    return lax.ppermute(value, axis, [(i, (i + by) % size) for i in range(size)])


def local(
    feats,
    weight,
    cotangent,
    labels,
    tile_vals,
    tile_row,
    tile_col,
    tile_count,
    hub_vals,
    hub_col,
    hub_dest,
    hub_row,
):
    n_blocks = lax.axis_size("blk")
    n_groups = lax.axis_size("grp")
    my_block = lax.axis_index("blk")
    my_group = lax.axis_index("grp")
    rows_dev = feats.shape[0]
    width = feats.shape[1]
    tile_size = tile_vals.shape[-1]
    row_tiles = rows_dev // tile_size
    slot_count = tile_vals.shape[3]
    hub_count = hub_vals.shape[2]
    capacity = max(2, hub_count // 4)
    highest = lax.Precision.HIGHEST
    dev_vals = tile_vals[0, 0]
    dev_rows = tile_row[0, 0]
    dev_cols = tile_col[0, 0]
    dev_count = tile_count[0, 0]
    tile_range = jnp.arange(row_tiles, dtype=jnp.int32)
    slot_range = jnp.arange(slot_count, dtype=jnp.int32)
    proj = jnp.dot(feats, weight, preferred_element_type=jnp.float32).astype(jnp.bfloat16)
    own_panel = proj.reshape(row_tiles, tile_size, width)

    def block_parts(source):
        blk_vals = lax.dynamic_index_in_dim(dev_vals, source, 0, keepdims=False)
        blk_rows = lax.dynamic_index_in_dim(dev_rows, source, 0, keepdims=False)
        blk_cols = lax.dynamic_index_in_dim(dev_cols, source, 0, keepdims=False)
        blk_count = lax.dynamic_index_in_dim(dev_count, source, 0, keepdims=False)
        live_mask = (slot_range < blk_count).astype(jnp.float32)
        return (blk_vals, blk_rows, blk_cols, live_mask)

    def forward_block(source, panel_now):
        blk_vals, blk_rows, blk_cols, live_mask = block_parts(source)
        picked = jnp.take(panel_now, blk_cols, axis=0)
        product = jnp.einsum("tij,tjf->tif", blk_vals, picked, preferred_element_type=jnp.float32)
        placing = (blk_rows[:, None] == tile_range[None, :]).astype(jnp.float32) * live_mask[
            :, None
        ]
        return jnp.einsum("tr,tif->rif", placing, product, precision=highest)

    def backward_block(target, grad_tiles):
        blk_vals, blk_rows, blk_cols, live_mask = block_parts(target)
        picked = jnp.take(grad_tiles, blk_rows, axis=0)
        product = jnp.einsum("tij,tif->tjf", blk_vals, picked, preferred_element_type=jnp.float32)
        placing = (blk_cols[:, None] == tile_range[None, :]).astype(jnp.float32) * live_mask[
            :, None
        ]
        return jnp.einsum("tr,tjf->rjf", placing, product, precision=highest)

    agg_sum = forward_block(my_block, own_panel)

    def forward_turn(k, carry):
        panel_now, running = carry
        panel_now = shifted(panel_now, "blk", 1)
        source = (my_block - k) % n_blocks
        return (panel_now, running + forward_block(source, panel_now))

    _, agg_sum = lax.fori_loop(1, n_blocks, forward_turn, (own_panel, agg_sum))
    dest_all = hub_dest[:, 0, :, 0]
    hub_rows_all = hub_row[:, 0, :]
    hub_range = jnp.arange(hub_count, dtype=jnp.int32)
    earlier = hub_range[None, :] < hub_range[:, None]
    same_dest = dest_all[:, :, None] == dest_all[:, None, :]
    rank_all = jnp.sum((same_dest & earlier[None, :, :]).astype(jnp.int32), axis=-1)
    my_dest = lax.dynamic_index_in_dim(dest_all, my_group, 0, keepdims=False)
    my_rank = lax.dynamic_index_in_dim(rank_all, my_group, 0, keepdims=False)
    slot_of = my_dest * capacity + my_rank
    send_place = (
        slot_of[:, None] == jnp.arange(n_groups * capacity, dtype=jnp.int32)[None, :]
    ).astype(jnp.float32)
    hub_tiles = hub_vals[0, 0]
    hub_cols = hub_col[0, 0]
    hub_src = jnp.take(own_panel, hub_cols, axis=0)
    hub_part = jnp.einsum("hij,hjf->hif", hub_tiles, hub_src, preferred_element_type=jnp.float32)
    send_buf = jnp.einsum("hs,hif->sif", send_place, hub_part, precision=highest)
    send_buf = send_buf.reshape(n_groups, capacity, tile_size, width)
    received = lax.all_to_all(send_buf, "grp", split_axis=0, concat_axis=0, tiled=True)
    chosen = (dest_all == my_group).astype(jnp.float32)
    slot_hot = (rank_all[..., None] == jnp.arange(capacity, dtype=jnp.int32)).astype(
        jnp.float32
    ) * chosen[..., None]
    row_hot = (hub_rows_all[..., None] == tile_range).astype(jnp.float32)
    routing = jnp.einsum("shc,shr->scr", slot_hot, row_hot, precision=highest)
    agg_sum = agg_sum + jnp.einsum("scr,scif->rif", routing, received, precision=highest)
    agg_rows = agg_sum.reshape(rows_dev, width)
    layer_out = jax.nn.silu(agg_rows).astype(jnp.bfloat16)
    sigmoid_z = jax.nn.sigmoid(agg_rows)
    slope = sigmoid_z * (1.0 + agg_rows * (1.0 - sigmoid_z))
    keep = (labels >= 0).astype(jnp.float32)[:, None]
    grad_agg = (cotangent.astype(jnp.float32) * keep * slope).astype(jnp.bfloat16)
    grad_tiles = grad_agg.reshape(row_tiles, tile_size, width)
    grad_sum = backward_block((my_block + n_blocks - 1) % n_blocks, grad_tiles)

    def backward_turn(k, running):
        running = shifted(running, "blk", 1)
        return running + backward_block((my_block + n_blocks - 1 - k) % n_blocks, grad_tiles)

    grad_sum = lax.fori_loop(1, n_blocks, backward_turn, grad_sum)
    back_send = jnp.einsum(
        "scr,rif->scif",
        routing.astype(jnp.bfloat16),
        grad_tiles,
        preferred_element_type=jnp.float32,
    ).astype(jnp.bfloat16)
    back_recv = lax.all_to_all(back_send, "grp", split_axis=0, concat_axis=0, tiled=True)
    back_flat = back_recv.reshape(n_groups * capacity, tile_size, width)
    own_pick = jnp.einsum(
        "hs,sif->hif",
        send_place.astype(jnp.bfloat16),
        back_flat,
        preferred_element_type=jnp.float32,
    ).astype(jnp.bfloat16)
    hub_back = jnp.einsum("hij,hif->hjf", hub_tiles, own_pick, preferred_element_type=jnp.float32)
    col_hot = (hub_cols[:, None] == tile_range[None, :]).astype(jnp.float32)
    grad_sum = grad_sum + jnp.einsum("hr,hjf->rjf", col_hot, hub_back, precision=highest)
    grad_rows = grad_sum.reshape(rows_dev, width).astype(jnp.bfloat16)
    weight_term = lax.dot_general(
        feats, grad_rows, (((0,), (0,)), ((), ())), preferred_element_type=jnp.float32
    )
    grad_scale = 1.0 / math.sqrt(rows_dev * n_blocks * n_groups)
    grad_weight = lax.psum(weight_term, ("grp", "blk")) * grad_scale
    grad_feats = lax.dot_general(
        grad_rows, weight, (((1,), (1,)), ((), ())), preferred_element_type=jnp.float32
    ).astype(jnp.bfloat16)
    return (layer_out, grad_feats, grad_weight)


def solution(mesh):
    in_specs = (
        P(("grp", "blk"), None),
        P(),
        P(("grp", "blk"), None),
        P(("grp", "blk")),
        P("grp", "blk", None, None, None, None),
        P("grp", "blk", None, None),
        P("grp", "blk", None, None),
        P("grp", "blk", None),
        P("grp", "blk", None, None, None),
        P("grp", "blk", None),
        P(None, "blk", None, None),
        P(None, "blk", None),
    )
    out_specs = (P(("grp", "blk"), None), P(("grp", "blk"), None), P())
    return jax.shard_map(local, mesh=mesh, in_specs=in_specs, out_specs=out_specs, check_vma=False)
```

profile of v0, /device:TPU:1, one launch (start us, length us, event | category | flops | bytes accessed | tf_op | source)
XLA Modules:
  0.0 958.8 jit_solution(11379729683561159299)
XLA Ops:
  31.5 6.6 all-to-all-start
  51.4 313.8 %while.34 = (s32[]{:T(128)}, bf16[8,128,256]{2,1,0:T(8,128)(2,1)S(1)}, f32[8,128,256]{2,0,1:T(8,128)}, s32[]{:T(128)}, s32[16,32]{1,0:T(8,128)}, /*index=5*/s32[...) while((s32[]{:T(128)}, ...), condition=%wide.region_1.3_spmd.clone, body=%wide.region_0.2_spmd.clone.sunk | while | flops 370411264 | bytes 29365836 | solution.py:82
  73.1 11.3 %collective-permute-done = bf16[8,128,256]{2,1,0:T(8,128)(2,1)S(1)} collective-permute-done((bf16[8,128,256]{2,1,0:T(8,128)(2,1)S(1)}, bf16[8,128,256]{2,1,0:T(8,128)(2,1)S(1)}, u32[]{:S(2)}, u32[]{:S(2)}) %collective-permute-start) | collective-permute-done | bytes 524320 | tf_op jit(solution)/shard_map/while/body/eval_jaxpr/ppermute | solution.py:10
  95.4 14.3 %collective-permute-done = bf16[8,128,256]{2,1,0:T(8,128)(2,1)S(1)} collective-permute-done((bf16[8,128,256]{2,1,0:T(8,128)(2,1)S(1)}, bf16[8,128,256]{2,1,0:T(8,128)(2,1)S(1)}, u32[]{:S(2)}, u32[]{:S(2)}) %collective-permute-start) | collective-permute-done | bytes 524320 | tf_op jit(solution)/shard_map/while/body/eval_jaxpr/ppermute | solution.py:10
  120.7 9.6 collective-permute-done
  141.3 9.6 collective-permute-done
  161.9 9.6 collective-permute-done
  182.5 9.6 collective-permute-done
  203.1 9.6 collective-permute-done
  223.7 9.6 collective-permute-done
  244.3 9.6 collective-permute-done
  264.8 9.6 collective-permute-done
  285.4 9.6 collective-permute-done
  306.0 9.6 collective-permute-done
  326.6 9.6 collective-permute-done
  347.2 9.6 collective-permute-done
  365.1 15.8 %fusion.65 = f32[8,128,256]{2,0,1:T(8,128)S(1)} fusion(f32[8,128,256]{2,0,1:T(8,128)} %get-tuple-element.494, f32[8,4,128,256]{3,1,2,0:T(4,128)} %all-to-all-done, f32[8,4,8]{2,1,0:T(4,128)S(1)} %fusion.89), kind=kOutput, calls=%fused_computation.79 | convolution fusion | flops 100925440 | bytes 6292480 | tf_op jit(solution)/shard_map/scr,scif->rif/dot_general | solution.py:108
  389.4 21.2 %copy.51 = bf16[1,1,16,32,128,128]{4,5,3,2,1,0:T(8,128)(2,1)} copy(bf16[1,1,16,32,128,128]{5,4,3,2,1,0:T(8,128)(2,1)} %bitcast.174) | data formatting | bytes 33554432 | tf_op args[4]
  425.9 365.8 %while.35 = (s32[]{:T(128)}, f32[8,128,256]{2,0,1:T(8,128)}, s32[]{:T(128)}, s32[16,32]{1,0:T(8,128)}, s32[16]{0:T(128)S(1)}, /*index=5*/bf16[16,32,128,128]{2,3...) while((s32[]{:T(128)}, f32[8,128,256]{2,0,1:T(8,128)}, ...), condition=%wide.region_4.6_spmd.clone, body=%wide.region_3.5_spmd.clone.sunk | while | flops 370411264 | bytes 22025748 | solution.py:122
  431.3 8.0 collective-permute-done.1
  439.2 6.6 fusion.170
  452.3 11.6 %collective-permute-done.1 = f32[8,128,256]{2,0,1:T(8,128)} collective-permute-done((f32[8,128,256]{2,0,1:T(8,128)}, f32[8,128,256]{2,0,1:T(8,128)}, u32[]{:S(2)}, u32[]{:S(2)}) %collective-permute-start.1) | collective-permute-done | bytes 1048608 | tf_op jit(solution)/shard_map/while/body/eval_jaxpr/ppermute | solution.py:10
  463.9 6.6 fusion.170
  475.8 12.8 %collective-permute-done.1 = f32[8,128,256]{2,0,1:T(8,128)} collective-permute-done((f32[8,128,256]{2,0,1:T(8,128)}, f32[8,128,256]{2,0,1:T(8,128)}, u32[]{:S(2)}, u32[]{:S(2)}) %collective-permute-start.1) | collective-permute-done | bytes 1048608 | tf_op jit(solution)/shard_map/while/body/eval_jaxpr/ppermute | solution.py:10
  488.6 6.6 fusion.170
  500.5 12.8 %collective-permute-done.1 = f32[8,128,256]{2,0,1:T(8,128)} collective-permute-done((f32[8,128,256]{2,0,1:T(8,128)}, f32[8,128,256]{2,0,1:T(8,128)}, u32[]{:S(2)}, u32[]{:S(2)}) %collective-permute-start.1) | collective-permute-done | bytes 1048608 | tf_op jit(solution)/shard_map/while/body/eval_jaxpr/ppermute | solution.py:10
  513.3 6.6 fusion.170
  525.2 12.8 %collective-permute-done.1 = f32[8,128,256]{2,0,1:T(8,128)} collective-permute-done((f32[8,128,256]{2,0,1:T(8,128)}, f32[8,128,256]{2,0,1:T(8,128)}, u32[]{:S(2)}, u32[]{:S(2)}) %collective-permute-start.1) | collective-permute-done | bytes 1048608 | tf_op jit(solution)/shard_map/while/body/eval_jaxpr/ppermute | solution.py:10
  538.1 6.6 fusion.170
  550.0 12.8 %collective-permute-done.1 = f32[8,128,256]{2,0,1:T(8,128)} collective-permute-done((f32[8,128,256]{2,0,1:T(8,128)}, f32[8,128,256]{2,0,1:T(8,128)}, u32[]{:S(2)}, u32[]{:S(2)}) %collective-permute-start.1) | collective-permute-done | bytes 1048608 | tf_op jit(solution)/shard_map/while/body/eval_jaxpr/ppermute | solution.py:10
  562.8 6.6 fusion.170
  574.7 12.8 %collective-permute-done.1 = f32[8,128,256]{2,0,1:T(8,128)} collective-permute-done((f32[8,128,256]{2,0,1:T(8,128)}, f32[8,128,256]{2,0,1:T(8,128)}, u32[]{:S(2)}, u32[]{:S(2)}) %collective-permute-start.1) | collective-permute-done | bytes 1048608 | tf_op jit(solution)/shard_map/while/body/eval_jaxpr/ppermute | solution.py:10
  587.5 6.6 fusion.170
  599.4 12.8 %collective-permute-done.1 = f32[8,128,256]{2,0,1:T(8,128)} collective-permute-done((f32[8,128,256]{2,0,1:T(8,128)}, f32[8,128,256]{2,0,1:T(8,128)}, u32[]{:S(2)}, u32[]{:S(2)}) %collective-permute-start.1) | collective-permute-done | bytes 1048608 | tf_op jit(solution)/shard_map/while/body/eval_jaxpr/ppermute | solution.py:10
  612.2 6.6 fusion.170
  624.1 12.8 %collective-permute-done.1 = f32[8,128,256]{2,0,1:T(8,128)} collective-permute-done((f32[8,128,256]{2,0,1:T(8,128)}, f32[8,128,256]{2,0,1:T(8,128)}, u32[]{:S(2)}, u32[]{:S(2)}) %collective-permute-start.1) | collective-permute-done | bytes 1048608 | tf_op jit(solution)/shard_map/while/body/eval_jaxpr/ppermute | solution.py:10
  636.9 6.6 fusion.170
  648.8 12.8 %collective-permute-done.1 = f32[8,128,256]{2,0,1:T(8,128)} collective-permute-done((f32[8,128,256]{2,0,1:T(8,128)}, f32[8,128,256]{2,0,1:T(8,128)}, u32[]{:S(2)}, u32[]{:S(2)}) %collective-permute-start.1) | collective-permute-done | bytes 1048608 | tf_op jit(solution)/shard_map/while/body/eval_jaxpr/ppermute | solution.py:10
  661.6 6.6 fusion.170
  673.5 12.8 %collective-permute-done.1 = f32[8,128,256]{2,0,1:T(8,128)} collective-permute-done((f32[8,128,256]{2,0,1:T(8,128)}, f32[8,128,256]{2,0,1:T(8,128)}, u32[]{:S(2)}, u32[]{:S(2)}) %collective-permute-start.1) | collective-permute-done | bytes 1048608 | tf_op jit(solution)/shard_map/while/body/eval_jaxpr/ppermute | solution.py:10
  686.3 6.6 fusion.170
  698.2 12.8 %collective-permute-done.1 = f32[8,128,256]{2,0,1:T(8,128)} collective-permute-done((f32[8,128,256]{2,0,1:T(8,128)}, f32[8,128,256]{2,0,1:T(8,128)}, u32[]{:S(2)}, u32[]{:S(2)}) %collective-permute-start.1) | collective-permute-done | bytes 1048608 | tf_op jit(solution)/shard_map/while/body/eval_jaxpr/ppermute | solution.py:10
  711.0 6.6 fusion.170
  722.9 12.8 %collective-permute-done.1 = f32[8,128,256]{2,0,1:T(8,128)} collective-permute-done((f32[8,128,256]{2,0,1:T(8,128)}, f32[8,128,256]{2,0,1:T(8,128)}, u32[]{:S(2)}, u32[]{:S(2)}) %collective-permute-start.1) | collective-permute-done | bytes 1048608 | tf_op jit(solution)/shard_map/while/body/eval_jaxpr/ppermute | solution.py:10
  735.7 6.6 fusion.170
  747.6 12.8 %collective-permute-done.1 = f32[8,128,256]{2,0,1:T(8,128)} collective-permute-done((f32[8,128,256]{2,0,1:T(8,128)}, f32[8,128,256]{2,0,1:T(8,128)}, u32[]{:S(2)}, u32[]{:S(2)}) %collective-permute-start.1) | collective-permute-done | bytes 1048608 | tf_op jit(solution)/shard_map/while/body/eval_jaxpr/ppermute | solution.py:10
  772.3 12.8 %collective-permute-done.1 = f32[8,128,256]{2,0,1:T(8,128)} collective-permute-done((f32[8,128,256]{2,0,1:T(8,128)}, f32[8,128,256]{2,0,1:T(8,128)}, u32[]{:S(2)}, u32[]{:S(2)}) %collective-permute-start.1) | collective-permute-done | bytes 1048608 | tf_op jit(solution)/shard_map/while/body/eval_jaxpr/ppermute | solution.py:10
  796.8 153.1 %all-reduce.2.cloned.1.call-done = f32[256,256]{0,1:T(8,128)} async-done(((f32[256,256]{0,1:T(8,128)}), f32[256,256]{0,1:T(8,128)}) %all-reduce.2.cloned.1.call-update) | async-done | bytes 262160 | tf_op jit(solution)/shard_map/psum | solution.py:145
  (400 shorter events, 334.3 us)
Async XLA Ops:
  7.2 3.4 copy-start
  12.5 3.2 copy-start.6
  31.5 333.6 %all-to-all-start = ((f32[8,4,128,256]{3,1,2,0:T(4,128)}), f32[8,4,128,256]{3,1,2,0:T(4,128)}, u32[]{:S(2)}, u32[]{:S(2)}) async-start(f32[8,4,128,256]{3,1,2,0:T(4,128)} %copy.55), calls=%async_computation | async-start | bytes 8388608 | tf_op jit(solution)/shard_map/all_to_all | solution.py:101
  39.6 3.4 copy-start.7
  39.7 3.4 copy-start.10
  51.4 8.3 collective-permute-start
  60.3 2.1 copy-start.1
  68.0 16.4 %collective-permute-start = (bf16[8,128,256]{2,1,0:T(8,128)(2,1)S(1)}, bf16[8,128,256]{2,1,0:T(8,128)(2,1)S(1)}, u32[]{:S(2)}, u32[]{:S(2)}) collective-permute-start(bf16[8,128,256]{2,1,0:T(8,128)(2,1)S(1)} %get-tuple-element.727), channel_id=1, source_target_pairs={{0,1},{1,2},{2,3},{3,4},{4,5},{5,6},{6,7},{7,8},{8,9},{9,10},{10,1... | collective-permute-start | bytes 1572872 | tf_op jit(solution)/shard_map/while/body/eval_jaxpr/ppermute | solution.py:10
  92.8 16.9 %collective-permute-start = (bf16[8,128,256]{2,1,0:T(8,128)(2,1)S(1)}, bf16[8,128,256]{2,1,0:T(8,128)(2,1)S(1)}, u32[]{:S(2)}, u32[]{:S(2)}) collective-permute-start(bf16[8,128,256]{2,1,0:T(8,128)(2,1)S(1)} %get-tuple-element.727), channel_id=1, source_target_pairs={{0,1},{1,2},{2,3},{3,4},{4,5},{5,6},{6,7},{7,8},{8,9},{9,10},{10,1... | collective-permute-start | bytes 1572872 | tf_op jit(solution)/shard_map/while/body/eval_jaxpr/ppermute | solution.py:10
  110.4 2.1 copy-start.1
  118.1 12.2 %collective-permute-start = (bf16[8,128,256]{2,1,0:T(8,128)(2,1)S(1)}, bf16[8,128,256]{2,1,0:T(8,128)(2,1)S(1)}, u32[]{:S(2)}, u32[]{:S(2)}) collective-permute-start(bf16[8,128,256]{2,1,0:T(8,128)(2,1)S(1)} %get-tuple-element.727), channel_id=1, source_target_pairs={{0,1},{1,2},{2,3},{3,4},{4,5},{5,6},{6,7},{7,8},{8,9},{9,10},{10,1... | collective-permute-start | bytes 1572872 | tf_op jit(solution)/shard_map/while/body/eval_jaxpr/ppermute | solution.py:10
  138.7 12.2 %collective-permute-start = (bf16[8,128,256]{2,1,0:T(8,128)(2,1)S(1)}, bf16[8,128,256]{2,1,0:T(8,128)(2,1)S(1)}, u32[]{:S(2)}, u32[]{:S(2)}) collective-permute-start(bf16[8,128,256]{2,1,0:T(8,128)(2,1)S(1)} %get-tuple-element.727), channel_id=1, source_target_pairs={{0,1},{1,2},{2,3},{3,4},{4,5},{5,6},{6,7},{7,8},{8,9},{9,10},{10,1... | collective-permute-start | bytes 1572872 | tf_op jit(solution)/shard_map/while/body/eval_jaxpr/ppermute | solution.py:10
  151.6 2.1 copy-start.1
  159.3 12.2 %collective-permute-start = (bf16[8,128,256]{2,1,0:T(8,128)(2,1)S(1)}, bf16[8,128,256]{2,1,0:T(8,128)(2,1)S(1)}, u32[]{:S(2)}, u32[]{:S(2)}) collective-permute-start(bf16[8,128,256]{2,1,0:T(8,128)(2,1)S(1)} %get-tuple-element.727), channel_id=1, source_target_pairs={{0,1},{1,2},{2,3},{3,4},{4,5},{5,6},{6,7},{7,8},{8,9},{9,10},{10,1... | collective-permute-start | bytes 1572872 | tf_op jit(solution)/shard_map/while/body/eval_jaxpr/ppermute | solution.py:10
  172.2 2.1 copy-start.1
  179.9 12.2 %collective-permute-start = (bf16[8,128,256]{2,1,0:T(8,128)(2,1)S(1)}, bf16[8,128,256]{2,1,0:T(8,128)(2,1)S(1)}, u32[]{:S(2)}, u32[]{:S(2)}) collective-permute-start(bf16[8,128,256]{2,1,0:T(8,128)(2,1)S(1)} %get-tuple-element.727), channel_id=1, source_target_pairs={{0,1},{1,2},{2,3},{3,4},{4,5},{5,6},{6,7},{7,8},{8,9},{9,10},{10,1... | collective-permute-start | bytes 1572872 | tf_op jit(solution)/shard_map/while/body/eval_jaxpr/ppermute | solution.py:10
  200.4 12.2 %collective-permute-start = (bf16[8,128,256]{2,1,0:T(8,128)(2,1)S(1)}, bf16[8,128,256]{2,1,0:T(8,128)(2,1)S(1)}, u32[]{:S(2)}, u32[]{:S(2)}) collective-permute-start(bf16[8,128,256]{2,1,0:T(8,128)(2,1)S(1)} %get-tuple-element.727), channel_id=1, source_target_pairs={{0,1},{1,2},{2,3},{3,4},{4,5},{5,6},{6,7},{7,8},{8,9},{9,10},{10,1... | collective-permute-start | bytes 1572872 | tf_op jit(solution)/shard_map/while/body/eval_jaxpr/ppermute | solution.py:10
  213.4 2.1 copy-start.1
  221.0 12.2 %collective-permute-start = (bf16[8,128,256]{2,1,0:T(8,128)(2,1)S(1)}, bf16[8,128,256]{2,1,0:T(8,128)(2,1)S(1)}, u32[]{:S(2)}, u32[]{:S(2)}) collective-permute-start(bf16[8,128,256]{2,1,0:T(8,128)(2,1)S(1)} %get-tuple-element.727), channel_id=1, source_target_pairs={{0,1},{1,2},{2,3},{3,4},{4,5},{5,6},{6,7},{7,8},{8,9},{9,10},{10,1... | collective-permute-start | bytes 1572872 | tf_op jit(solution)/shard_map/while/body/eval_jaxpr/ppermute | solution.py:10
  233.9 2.1 copy-start.1
  241.6 12.2 %collective-permute-start = (bf16[8,128,256]{2,1,0:T(8,128)(2,1)S(1)}, bf16[8,128,256]{2,1,0:T(8,128)(2,1)S(1)}, u32[]{:S(2)}, u32[]{:S(2)}) collective-permute-start(bf16[8,128,256]{2,1,0:T(8,128)(2,1)S(1)} %get-tuple-element.727), channel_id=1, source_target_pairs={{0,1},{1,2},{2,3},{3,4},{4,5},{5,6},{6,7},{7,8},{8,9},{9,10},{10,1... | collective-permute-start | bytes 1572872 | tf_op jit(solution)/shard_map/while/body/eval_jaxpr/ppermute | solution.py:10
  262.2 12.2 %collective-permute-start = (bf16[8,128,256]{2,1,0:T(8,128)(2,1)S(1)}, bf16[8,128,256]{2,1,0:T(8,128)(2,1)S(1)}, u32[]{:S(2)}, u32[]{:S(2)}) collective-permute-start(bf16[8,128,256]{2,1,0:T(8,128)(2,1)S(1)} %get-tuple-element.727), channel_id=1, source_target_pairs={{0,1},{1,2},{2,3},{3,4},{4,5},{5,6},{6,7},{7,8},{8,9},{9,10},{10,1... | collective-permute-start | bytes 1572872 | tf_op jit(solution)/shard_map/while/body/eval_jaxpr/ppermute | solution.py:10
  275.1 2.1 copy-start.1
  282.8 12.2 %collective-permute-start = (bf16[8,128,256]{2,1,0:T(8,128)(2,1)S(1)}, bf16[8,128,256]{2,1,0:T(8,128)(2,1)S(1)}, u32[]{:S(2)}, u32[]{:S(2)}) collective-permute-start(bf16[8,128,256]{2,1,0:T(8,128)(2,1)S(1)} %get-tuple-element.727), channel_id=1, source_target_pairs={{0,1},{1,2},{2,3},{3,4},{4,5},{5,6},{6,7},{7,8},{8,9},{9,10},{10,1... | collective-permute-start | bytes 1572872 | tf_op jit(solution)/shard_map/while/body/eval_jaxpr/ppermute | solution.py:10
  295.7 2.1 copy-start.1
  303.4 12.2 %collective-permute-start = (bf16[8,128,256]{2,1,0:T(8,128)(2,1)S(1)}, bf16[8,128,256]{2,1,0:T(8,128)(2,1)S(1)}, u32[]{:S(2)}, u32[]{:S(2)}) collective-permute-start(bf16[8,128,256]{2,1,0:T(8,128)(2,1)S(1)} %get-tuple-element.727), channel_id=1, source_target_pairs={{0,1},{1,2},{2,3},{3,4},{4,5},{5,6},{6,7},{7,8},{8,9},{9,10},{10,1... | collective-permute-start | bytes 1572872 | tf_op jit(solution)/shard_map/while/body/eval_jaxpr/ppermute | solution.py:10
  324.0 12.2 %collective-permute-start = (bf16[8,128,256]{2,1,0:T(8,128)(2,1)S(1)}, bf16[8,128,256]{2,1,0:T(8,128)(2,1)S(1)}, u32[]{:S(2)}, u32[]{:S(2)}) collective-permute-start(bf16[8,128,256]{2,1,0:T(8,128)(2,1)S(1)} %get-tuple-element.727), channel_id=1, source_target_pairs={{0,1},{1,2},{2,3},{3,4},{4,5},{5,6},{6,7},{7,8},{8,9},{9,10},{10,1... | collective-permute-start | bytes 1572872 | tf_op jit(solution)/shard_map/while/body/eval_jaxpr/ppermute | solution.py:10
  344.6 12.2 %collective-permute-start = (bf16[8,128,256]{2,1,0:T(8,128)(2,1)S(1)}, bf16[8,128,256]{2,1,0:T(8,128)(2,1)S(1)}, u32[]{:S(2)}, u32[]{:S(2)}) collective-permute-start(bf16[8,128,256]{2,1,0:T(8,128)(2,1)S(1)} %get-tuple-element.727), channel_id=1, source_target_pairs={{0,1},{1,2},{2,3},{3,4},{4,5},{5,6},{6,7},{7,8},{8,9},{9,10},{10,1... | collective-permute-start | bytes 1572872 | tf_op jit(solution)/shard_map/while/body/eval_jaxpr/ppermute | solution.py:10
  357.5 2.1 copy-start.1
  385.7 36.3 %all-to-all-start.1 = ((bf16[8,4,128,256]{3,2,1,0:T(8,128)(2,1)}), bf16[8,4,128,256]{3,2,1,0:T(8,128)(2,1)S(1)}, u32[]{:S(2)}, u32[]{:S(2)}) async-start(bf16[8,4,128,256]{3,2,1,0:T(8,128)(2,1)} %copy.62), calls=%async_computation.1 | async-start | bytes 4194304 | tf_op jit(solution)/shard_map/all_to_all | solution.py:129
  389.3 560.6 %all-reduce.2.cloned.1.call-start = ((), (), s32[]{:S(2)}) async-start(), calls=%async_computation.2 | async-start | bytes 524288 | tf_op jit(solution)/shard_map/psum | solution.py:145
  425.9 365.8 %copy-start.9 = (s32[1,1,16]{2,1,0:T(1,128)S(1)}, s32[1,1,16]{2,1,0:T(1,128)}, u32[]{:S(2)}) copy-start(s32[1,1,16]{2,1,0:T(1,128)} %param.27) | copy-start | bytes 196
  425.9 13.3 %collective-permute-start.1 = (f32[8,128,256]{2,0,1:T(8,128)}, f32[8,128,256]{2,0,1:T(8,128)}, u32[]{:S(2)}, u32[]{:S(2)}) collective-permute-start(f32[8,128,256]{2,0,1:T(8,128)} %get-tuple-element.763), channel_id=1, source_target_pairs={{0,1},{1,2},{2,3},{3,4},{4,5},{5,6},{6,7},{7,8},{8,9},{9,10},{10,1... | collective-permute-start | bytes 3145736 | tf_op jit(solution)/shard_map/while/body/eval_jaxpr/ppermute | solution.py:10
  445.8 18.2 %collective-permute-start.1 = (f32[8,128,256]{2,0,1:T(8,128)}, f32[8,128,256]{2,0,1:T(8,128)}, u32[]{:S(2)}, u32[]{:S(2)}) collective-permute-start(f32[8,128,256]{2,0,1:T(8,128)} %get-tuple-element.763), channel_id=1, source_target_pairs={{0,1},{1,2},{2,3},{3,4},{4,5},{5,6},{6,7},{7,8},{8,9},{9,10},{10,1... | collective-permute-start | bytes 3145736 | tf_op jit(solution)/shard_map/while/body/eval_jaxpr/ppermute | solution.py:10
  470.5 18.2 %collective-permute-start.1 = (f32[8,128,256]{2,0,1:T(8,128)}, f32[8,128,256]{2,0,1:T(8,128)}, u32[]{:S(2)}, u32[]{:S(2)}) collective-permute-start(f32[8,128,256]{2,0,1:T(8,128)} %get-tuple-element.763), channel_id=1, source_target_pairs={{0,1},{1,2},{2,3},{3,4},{4,5},{5,6},{6,7},{7,8},{8,9},{9,10},{10,1... | collective-permute-start | bytes 3145736 | tf_op jit(solution)/shard_map/while/body/eval_jaxpr/ppermute | solution.py:10
  495.2 18.2 %collective-permute-start.1 = (f32[8,128,256]{2,0,1:T(8,128)}, f32[8,128,256]{2,0,1:T(8,128)}, u32[]{:S(2)}, u32[]{:S(2)}) collective-permute-start(f32[8,128,256]{2,0,1:T(8,128)} %get-tuple-element.763), channel_id=1, source_target_pairs={{0,1},{1,2},{2,3},{3,4},{4,5},{5,6},{6,7},{7,8},{8,9},{9,10},{10,1... | collective-permute-start | bytes 3145736 | tf_op jit(solution)/shard_map/while/body/eval_jaxpr/ppermute | solution.py:10
  519.9 18.2 %collective-permute-start.1 = (f32[8,128,256]{2,0,1:T(8,128)}, f32[8,128,256]{2,0,1:T(8,128)}, u32[]{:S(2)}, u32[]{:S(2)}) collective-permute-start(f32[8,128,256]{2,0,1:T(8,128)} %get-tuple-element.763), channel_id=1, source_target_pairs={{0,1},{1,2},{2,3},{3,4},{4,5},{5,6},{6,7},{7,8},{8,9},{9,10},{10,1... | collective-permute-start | bytes 3145736 | tf_op jit(solution)/shard_map/while/body/eval_jaxpr/ppermute | solution.py:10
  544.6 18.2 %collective-permute-start.1 = (f32[8,128,256]{2,0,1:T(8,128)}, f32[8,128,256]{2,0,1:T(8,128)}, u32[]{:S(2)}, u32[]{:S(2)}) collective-permute-start(f32[8,128,256]{2,0,1:T(8,128)} %get-tuple-element.763), channel_id=1, source_target_pairs={{0,1},{1,2},{2,3},{3,4},{4,5},{5,6},{6,7},{7,8},{8,9},{9,10},{10,1... | collective-permute-start | bytes 3145736 | tf_op jit(solution)/shard_map/while/body/eval_jaxpr/ppermute | solution.py:10
  569.3 18.2 %collective-permute-start.1 = (f32[8,128,256]{2,0,1:T(8,128)}, f32[8,128,256]{2,0,1:T(8,128)}, u32[]{:S(2)}, u32[]{:S(2)}) collective-permute-start(f32[8,128,256]{2,0,1:T(8,128)} %get-tuple-element.763), channel_id=1, source_target_pairs={{0,1},{1,2},{2,3},{3,4},{4,5},{5,6},{6,7},{7,8},{8,9},{9,10},{10,1... | collective-permute-start | bytes 3145736 | tf_op jit(solution)/shard_map/while/body/eval_jaxpr/ppermute | solution.py:10
  594.0 18.2 %collective-permute-start.1 = (f32[8,128,256]{2,0,1:T(8,128)}, f32[8,128,256]{2,0,1:T(8,128)}, u32[]{:S(2)}, u32[]{:S(2)}) collective-permute-start(f32[8,128,256]{2,0,1:T(8,128)} %get-tuple-element.763), channel_id=1, source_target_pairs={{0,1},{1,2},{2,3},{3,4},{4,5},{5,6},{6,7},{7,8},{8,9},{9,10},{10,1... | collective-permute-start | bytes 3145736 | tf_op jit(solution)/shard_map/while/body/eval_jaxpr/ppermute | solution.py:10
  618.7 18.2 %collective-permute-start.1 = (f32[8,128,256]{2,0,1:T(8,128)}, f32[8,128,256]{2,0,1:T(8,128)}, u32[]{:S(2)}, u32[]{:S(2)}) collective-permute-start(f32[8,128,256]{2,0,1:T(8,128)} %get-tuple-element.763), channel_id=1, source_target_pairs={{0,1},{1,2},{2,3},{3,4},{4,5},{5,6},{6,7},{7,8},{8,9},{9,10},{10,1... | collective-permute-start | bytes 3145736 | tf_op jit(solution)/shard_map/while/body/eval_jaxpr/ppermute | solution.py:10
  643.5 18.2 %collective-permute-start.1 = (f32[8,128,256]{2,0,1:T(8,128)}, f32[8,128,256]{2,0,1:T(8,128)}, u32[]{:S(2)}, u32[]{:S(2)}) collective-permute-start(f32[8,128,256]{2,0,1:T(8,128)} %get-tuple-element.763), channel_id=1, source_target_pairs={{0,1},{1,2},{2,3},{3,4},{4,5},{5,6},{6,7},{7,8},{8,9},{9,10},{10,1... | collective-permute-start | bytes 3145736 | tf_op jit(solution)/shard_map/while/body/eval_jaxpr/ppermute | solution.py:10
  668.2 18.2 %collective-permute-start.1 = (f32[8,128,256]{2,0,1:T(8,128)}, f32[8,128,256]{2,0,1:T(8,128)}, u32[]{:S(2)}, u32[]{:S(2)}) collective-permute-start(f32[8,128,256]{2,0,1:T(8,128)} %get-tuple-element.763), channel_id=1, source_target_pairs={{0,1},{1,2},{2,3},{3,4},{4,5},{5,6},{6,7},{7,8},{8,9},{9,10},{10,1... | collective-permute-start | bytes 3145736 | tf_op jit(solution)/shard_map/while/body/eval_jaxpr/ppermute | solution.py:10
  692.9 18.2 %collective-permute-start.1 = (f32[8,128,256]{2,0,1:T(8,128)}, f32[8,128,256]{2,0,1:T(8,128)}, u32[]{:S(2)}, u32[]{:S(2)}) collective-permute-start(f32[8,128,256]{2,0,1:T(8,128)} %get-tuple-element.763), channel_id=1, source_target_pairs={{0,1},{1,2},{2,3},{3,4},{4,5},{5,6},{6,7},{7,8},{8,9},{9,10},{10,1... | collective-permute-start | bytes 3145736 | tf_op jit(solution)/shard_map/while/body/eval_jaxpr/ppermute | solution.py:10
  717.6 18.2 %collective-permute-start.1 = (f32[8,128,256]{2,0,1:T(8,128)}, f32[8,128,256]{2,0,1:T(8,128)}, u32[]{:S(2)}, u32[]{:S(2)}) collective-permute-start(f32[8,128,256]{2,0,1:T(8,128)} %get-tuple-element.763), channel_id=1, source_target_pairs={{0,1},{1,2},{2,3},{3,4},{4,5},{5,6},{6,7},{7,8},{8,9},{9,10},{10,1... | collective-permute-start | bytes 3145736 | tf_op jit(solution)/shard_map/while/body/eval_jaxpr/ppermute | solution.py:10
  742.3 18.2 %collective-permute-start.1 = (f32[8,128,256]{2,0,1:T(8,128)}, f32[8,128,256]{2,0,1:T(8,128)}, u32[]{:S(2)}, u32[]{:S(2)}) collective-permute-start(f32[8,128,256]{2,0,1:T(8,128)} %get-tuple-element.763), channel_id=1, source_target_pairs={{0,1},{1,2},{2,3},{3,4},{4,5},{5,6},{6,7},{7,8},{8,9},{9,10},{10,1... | collective-permute-start | bytes 3145736 | tf_op jit(solution)/shard_map/while/body/eval_jaxpr/ppermute | solution.py:10
  767.0 18.2 %collective-permute-start.1 = (f32[8,128,256]{2,0,1:T(8,128)}, f32[8,128,256]{2,0,1:T(8,128)}, u32[]{:S(2)}, u32[]{:S(2)}) collective-permute-start(f32[8,128,256]{2,0,1:T(8,128)} %get-tuple-element.763), channel_id=1, source_target_pairs={{0,1},{1,2},{2,3},{3,4},{4,5},{5,6},{6,7},{7,8},{8,9},{9,10},{10,1... | collective-permute-start | bytes 3145736 | tf_op jit(solution)/shard_map/while/body/eval_jaxpr/ppermute | solution.py:10
  791.7 2.9 copy-start.3
  (24 other events, 33.1 us)
Sparse Core Ops, SparseCore 0:
  795.8 154.0 all-reduce.1
where the time goes:
time: 967 us; the launch traced here: 959 us
  waiting for transfers between devices  483 us (50%)
  matrix products  275 us (28%)
  local copies, waits for them, and re-layouts  122 us (13%)
  other arithmetic  46.4 us (5%)
  starting transfers between devices  16.2 us (2%)
  between operations  14.5 us (1%)
    ppermute x30, waiting for transfers between devices, shifted(): lax.ppermute(value, axis, [(i, (i + by) % size) for i in range(size)])  330 us
    psum x1, waiting for transfers between devices, local(): grad_weight = lax.psum(weight_term, ('grp', 'blk')) * grad_scale  153 us
    dot_general x16, matrix products, backward_block(): return jnp.einsum('tr,tjf->rjf', placing, product, precision=highest)  104 us
    dot_general x16, matrix products, forward_block(): return jnp.einsum('tr,tif->rif', placing, product, precision=highest)  72.6 us
    dot_general x16, matrix products, forward_block(): jnp.einsum('tij,tjf->tif', blk_vals, picked, preferred_element_type=jnp.f...  34.1 us
    dot_general x16, matrix products, backward_block(): jnp.einsum('tij,tif->tjf', blk_vals, picked, preferred_element_type=jnp.f...  32.7 us
    unnamed x20, local copies, waits for them, and re-layouts  22.8 us
    convert_element_type x32, other arithmetic, block_parts(): live_mask = (slot_range < blk_count).astype(jnp.float32)  20.7 us
  transfers between devices with their start and end apart: 33, of which 31 were waited for; matrix products, arithmetic and copies ran while one was open for 29% of the time, Pallas kernels for 0%

commit v1 on v0

--- a/solution.py
+++ b/solution.py
@@ -1,8 +1,16 @@
+import functools
 import math
 import jax
 import jax.numpy as jnp
 from jax import lax
 from jax.sharding import PartitionSpec as P
+
+
+def rounds_save(row_data, a_name):
+    return lax.all_gather(row_data, a_name).sum(axis=0)
+
+
+chunk_edit = functools.partial(rounds_save, a_name=("grp", "blk"))
 
 
 def shifted(value, axis, by):
@@ -142,7 +150,7 @@
         feats, grad_rows, (((0,), (0,)), ((), ())), preferred_element_type=jnp.float32
     )
     grad_scale = 1.0 / math.sqrt(rows_dev * n_blocks * n_groups)
-    grad_weight = lax.psum(weight_term, ("grp", "blk")) * grad_scale
+    grad_weight = chunk_edit(weight_term) * grad_scale
     grad_feats = lax.dot_general(
         grad_rows, weight, (((1,), (1,)), ((), ())), preferred_element_type=jnp.float32
     ).astype(jnp.bfloat16)

time: 967 us -> 1080 us (1.12)
  waiting for transfers between devices: 483 us -> 579 us
  local copies, waits for them, and re-layouts: 122 us -> 141 us
    all_gather x0 -> x1, waiting for transfers between devices: none -> 249 us  [rounds_save(): return lax.all_gather(row_data, a_name).sum(axis=0)]
    psum x1 -> x0, waiting for transfers between devices: 153 us -> none  [local(): grad_weight = lax.psum(weight_term, ('grp', 'blk')) * grad_scale]
    unnamed x20 -> x23, local copies, waits for them, and re-layouts: 22.8 us -> 42.5 us
  transfers between devices with their start and end apart: 33 -> 33, of which waited for: 31 -> 31; matrix products, arithmetic and copies ran while one was open for 29% -> 26% of each run, Pallas kernels for 0% -> 0%
where the time goes in v1:
time: 1080 us; the launch traced here: 1070 us
  waiting for transfers between devices  579 us (54%)
  matrix products  267 us (25%)
  local copies, waits for them, and re-layouts  141 us (13%)
  other arithmetic  49.6 us (5%)
  starting transfers between devices  16.5 us (2%)
  between operations  14.5 us (1%)
    ppermute x30, waiting for transfers between devices, shifted(): lax.ppermute(value, axis, [(i, (i + by) % size) for i in range(size)])  330 us
    all_gather x1, waiting for transfers between devices, rounds_save(): return lax.all_gather(row_data, a_name).sum(axis=0)  249 us
    dot_general x16, matrix products, backward_block(): return jnp.einsum('tr,tjf->rjf', placing, product, precision=highest)  104 us
    dot_general x16, matrix products, forward_block(): return jnp.einsum('tr,tif->rif', placing, product, precision=highest)  72.6 us
    unnamed x23, local copies, waits for them, and re-layouts  42.5 us
    dot_general x16, matrix products, forward_block(): jnp.einsum('tij,tjf->tif', blk_vals, picked, preferred_element_type=jnp.f...  34.1 us
    dot_general x16, matrix products, backward_block(): jnp.einsum('tij,tif->tjf', blk_vals, picked, preferred_element_type=jnp.f...  32.7 us
  transfers between devices with their start and end apart: 33, of which 31 were waited for; matrix products, arithmetic and copies ran while one was open for 26% of the time, Pallas kernels for 0%

profile of v1, /device:TPU:1, one launch (start us, length us, event | category | flops | bytes accessed | tf_op | source)
XLA Modules:
  0.0 1069.1 jit_solution(10728234638235846559)
XLA Ops:
  31.5 6.9 all-to-all-start
  51.5 313.7 %while.34 = (s32[]{:T(128)}, bf16[8,128,256]{2,1,0:T(8,128)(2,1)S(1)}, f32[8,128,256]{2,0,1:T(8,128)}, s32[]{:T(128)}, s32[16,32]{1,0:T(8,128)}, /*index=5*/s32[...) while((s32[]{:T(128)}, ...), condition=%wide.region_1.3_spmd.clone, body=%wide.region_0.2_spmd.clone.sunk | while | flops 370411264 | bytes 29365836 | solution.py:90
  73.2 11.3 %collective-permute-done = bf16[8,128,256]{2,1,0:T(8,128)(2,1)S(1)} collective-permute-done((bf16[8,128,256]{2,1,0:T(8,128)(2,1)S(1)}, bf16[8,128,256]{2,1,0:T(8,128)(2,1)S(1)}, u32[]{:S(2)}, u32[]{:S(2)}) %collective-permute-start) | collective-permute-done | bytes 524320 | tf_op jit(solution)/shard_map/while/body/eval_jaxpr/ppermute | solution.py:18
  95.5 14.4 %collective-permute-done = bf16[8,128,256]{2,1,0:T(8,128)(2,1)S(1)} collective-permute-done((bf16[8,128,256]{2,1,0:T(8,128)(2,1)S(1)}, bf16[8,128,256]{2,1,0:T(8,128)(2,1)S(1)}, u32[]{:S(2)}, u32[]{:S(2)}) %collective-permute-start) | collective-permute-done | bytes 524320 | tf_op jit(solution)/shard_map/while/body/eval_jaxpr/ppermute | solution.py:18
  120.9 9.6 collective-permute-done
  141.5 9.6 collective-permute-done
  162.1 9.6 collective-permute-done
  182.6 9.6 collective-permute-done
  203.2 9.6 collective-permute-done
  223.8 9.6 collective-permute-done
  244.4 9.6 collective-permute-done
  264.9 9.6 collective-permute-done
  285.5 9.6 collective-permute-done
  306.1 9.6 collective-permute-done
  326.7 9.6 collective-permute-done
  347.2 9.6 collective-permute-done
  365.2 7.2 fusion.65
  380.8 21.3 %copy.49 = bf16[1,1,16,32,128,128]{4,5,3,2,1,0:T(8,128)(2,1)} copy(bf16[1,1,16,32,128,128]{5,4,3,2,1,0:T(8,128)(2,1)} %bitcast.179) | data formatting | bytes 33554432 | tf_op args[4]
  417.4 366.3 %while.35 = (s32[]{:T(128)}, f32[8,128,256]{2,0,1:T(8,128)}, s32[]{:T(128)}, s32[16,32]{1,0:T(8,128)}, s32[16]{0:T(128)S(1)}, /*index=5*/bf16[16,32,128,128]{2,3...) while((s32[]{:T(128)}, f32[8,128,256]{2,0,1:T(8,128)}, ...), condition=%wide.region_4.6_spmd.clone, body=%wide.region_3.5_spmd.clone.sunk | while | flops 370411264 | bytes 22025748 | solution.py:130
  423.1 7.9 collective-permute-done.1
  431.0 6.6 fusion.170
  444.1 11.6 %collective-permute-done.1 = f32[8,128,256]{2,0,1:T(8,128)} collective-permute-done((f32[8,128,256]{2,0,1:T(8,128)}, f32[8,128,256]{2,0,1:T(8,128)}, u32[]{:S(2)}, u32[]{:S(2)}) %collective-permute-start.1) | collective-permute-done | bytes 1048608 | tf_op jit(solution)/shard_map/while/body/eval_jaxpr/ppermute | solution.py:18
  455.7 6.6 fusion.170
  467.6 12.8 %collective-permute-done.1 = f32[8,128,256]{2,0,1:T(8,128)} collective-permute-done((f32[8,128,256]{2,0,1:T(8,128)}, f32[8,128,256]{2,0,1:T(8,128)}, u32[]{:S(2)}, u32[]{:S(2)}) %collective-permute-start.1) | collective-permute-done | bytes 1048608 | tf_op jit(solution)/shard_map/while/body/eval_jaxpr/ppermute | solution.py:18
  480.4 6.6 fusion.170
  492.4 12.8 %collective-permute-done.1 = f32[8,128,256]{2,0,1:T(8,128)} collective-permute-done((f32[8,128,256]{2,0,1:T(8,128)}, f32[8,128,256]{2,0,1:T(8,128)}, u32[]{:S(2)}, u32[]{:S(2)}) %collective-permute-start.1) | collective-permute-done | bytes 1048608 | tf_op jit(solution)/shard_map/while/body/eval_jaxpr/ppermute | solution.py:18
  505.2 6.6 fusion.170
  517.1 12.8 %collective-permute-done.1 = f32[8,128,256]{2,0,1:T(8,128)} collective-permute-done((f32[8,128,256]{2,0,1:T(8,128)}, f32[8,128,256]{2,0,1:T(8,128)}, u32[]{:S(2)}, u32[]{:S(2)}) %collective-permute-start.1) | collective-permute-done | bytes 1048608 | tf_op jit(solution)/shard_map/while/body/eval_jaxpr/ppermute | solution.py:18
  529.9 6.6 fusion.170
  541.8 12.8 %collective-permute-done.1 = f32[8,128,256]{2,0,1:T(8,128)} collective-permute-done((f32[8,128,256]{2,0,1:T(8,128)}, f32[8,128,256]{2,0,1:T(8,128)}, u32[]{:S(2)}, u32[]{:S(2)}) %collective-permute-start.1) | collective-permute-done | bytes 1048608 | tf_op jit(solution)/shard_map/while/body/eval_jaxpr/ppermute | solution.py:18
  554.6 6.6 fusion.170
  566.5 12.8 %collective-permute-done.1 = f32[8,128,256]{2,0,1:T(8,128)} collective-permute-done((f32[8,128,256]{2,0,1:T(8,128)}, f32[8,128,256]{2,0,1:T(8,128)}, u32[]{:S(2)}, u32[]{:S(2)}) %collective-permute-start.1) | collective-permute-done | bytes 1048608 | tf_op jit(solution)/shard_map/while/body/eval_jaxpr/ppermute | solution.py:18
  591.2 12.8 %collective-permute-done.1 = f32[8,128,256]{2,0,1:T(8,128)} collective-permute-done((f32[8,128,256]{2,0,1:T(8,128)}, f32[8,128,256]{2,0,1:T(8,128)}, u32[]{:S(2)}, u32[]{:S(2)}) %collective-permute-start.1) | collective-permute-done | bytes 1048608 | tf_op jit(solution)/shard_map/while/body/eval_jaxpr/ppermute | solution.py:18
  604.0 6.6 fusion.170
  616.0 12.8 %collective-permute-done.1 = f32[8,128,256]{2,0,1:T(8,128)} collective-permute-done((f32[8,128,256]{2,0,1:T(8,128)}, f32[8,128,256]{2,0,1:T(8,128)}, u32[]{:S(2)}, u32[]{:S(2)}) %collective-permute-start.1) | collective-permute-done | bytes 1048608 | tf_op jit(solution)/shard_map/while/body/eval_jaxpr/ppermute | solution.py:18
  628.8 6.6 fusion.170
  640.7 12.8 %collective-permute-done.1 = f32[8,128,256]{2,0,1:T(8,128)} collective-permute-done((f32[8,128,256]{2,0,1:T(8,128)}, f32[8,128,256]{2,0,1:T(8,128)}, u32[]{:S(2)}, u32[]{:S(2)}) %collective-permute-start.1) | collective-permute-done | bytes 1048608 | tf_op jit(solution)/shard_map/while/body/eval_jaxpr/ppermute | solution.py:18
  653.5 6.6 fusion.170
  665.4 12.8 %collective-permute-done.1 = f32[8,128,256]{2,0,1:T(8,128)} collective-permute-done((f32[8,128,256]{2,0,1:T(8,128)}, f32[8,128,256]{2,0,1:T(8,128)}, u32[]{:S(2)}, u32[]{:S(2)}) %collective-permute-start.1) | collective-permute-done | bytes 1048608 | tf_op jit(solution)/shard_map/while/body/eval_jaxpr/ppermute | solution.py:18
  678.2 6.6 fusion.170
  690.1 12.8 %collective-permute-done.1 = f32[8,128,256]{2,0,1:T(8,128)} collective-permute-done((f32[8,128,256]{2,0,1:T(8,128)}, f32[8,128,256]{2,0,1:T(8,128)}, u32[]{:S(2)}, u32[]{:S(2)}) %collective-permute-start.1) | collective-permute-done | bytes 1048608 | tf_op jit(solution)/shard_map/while/body/eval_jaxpr/ppermute | solution.py:18
  714.9 12.8 %collective-permute-done.1 = f32[8,128,256]{2,0,1:T(8,128)} collective-permute-done((f32[8,128,256]{2,0,1:T(8,128)}, f32[8,128,256]{2,0,1:T(8,128)}, u32[]{:S(2)}, u32[]{:S(2)}) %collective-permute-start.1) | collective-permute-done | bytes 1048608 | tf_op jit(solution)/shard_map/while/body/eval_jaxpr/ppermute | solution.py:18
  727.7 6.6 fusion.170
  739.6 12.8 %collective-permute-done.1 = f32[8,128,256]{2,0,1:T(8,128)} collective-permute-done((f32[8,128,256]{2,0,1:T(8,128)}, f32[8,128,256]{2,0,1:T(8,128)}, u32[]{:S(2)}, u32[]{:S(2)}) %collective-permute-start.1) | collective-permute-done | bytes 1048608 | tf_op jit(solution)/shard_map/while/body/eval_jaxpr/ppermute | solution.py:18
  764.3 12.8 %collective-permute-done.1 = f32[8,128,256]{2,0,1:T(8,128)} collective-permute-done((f32[8,128,256]{2,0,1:T(8,128)}, f32[8,128,256]{2,0,1:T(8,128)}, u32[]{:S(2)}, u32[]{:S(2)}) %collective-permute-start.1) | collective-permute-done | bytes 1048608 | tf_op jit(solution)/shard_map/while/body/eval_jaxpr/ppermute | solution.py:18
  777.1 6.6 fusion.170
  788.8 248.6 %all-gather.3.cloned.1.call-done = f32[32768,256]{0,1:T(8,128)} async-done(((f32[256,256]{0,1:T(8,128)}), f32[32768,256]{0,1:T(8,128)}) %all-gather.3.cloned.1.call-update) | async-done | bytes 33554448 | tf_op jit(solution)/shard_map/all_gather | solution.py:10
  1037.4 19.6 %copy.72 = f32[32,8,128,256]{3,2,1,0:T(8,128)S(1)} copy(f32[32,8,128,256]{3,1,2,0:T(8,128)} %bitcast.181) | data formatting | bytes 67108864
  (404 shorter events, 343.9 us)
Async XLA Ops:
  7.2 3.4 copy-start
  12.5 3.2 copy-start.7
  31.5 7.6 copy-start.9
  31.5 9.6 copy-start.8
  31.5 9.6 copy-start.11
  31.5 333.7 %all-to-all-start = ((f32[8,4,128,256]{3,1,2,0:T(4,128)}), f32[8,4,128,256]{3,1,2,0:T(4,128)}, u32[]{:S(2)}, u32[]{:S(2)}) async-start(f32[8,4,128,256]{3,1,2,0:T(4,128)} %copy.53), calls=%async_computation | async-start | bytes 8388608 | tf_op jit(solution)/shard_map/all_to_all | solution.py:109
  51.5 8.3 collective-permute-start
  60.5 2.1 copy-start.2
  68.1 16.4 %collective-permute-start = (bf16[8,128,256]{2,1,0:T(8,128)(2,1)S(1)}, bf16[8,128,256]{2,1,0:T(8,128)(2,1)S(1)}, u32[]{:S(2)}, u32[]{:S(2)}) collective-permute-start(bf16[8,128,256]{2,1,0:T(8,128)(2,1)S(1)} %get-tuple-element.721), channel_id=1, source_target_pairs={{0,1},{1,2},{2,3},{3,4},{4,5},{5,6},{6,7},{7,8},{8,9},{9,10},{10,1... | collective-permute-start | bytes 1572872 | tf_op jit(solution)/shard_map/while/body/eval_jaxpr/ppermute | solution.py:18
  92.9 17.0 %collective-permute-start = (bf16[8,128,256]{2,1,0:T(8,128)(2,1)S(1)}, bf16[8,128,256]{2,1,0:T(8,128)(2,1)S(1)}, u32[]{:S(2)}, u32[]{:S(2)}) collective-permute-start(bf16[8,128,256]{2,1,0:T(8,128)(2,1)S(1)} %get-tuple-element.721), channel_id=1, source_target_pairs={{0,1},{1,2},{2,3},{3,4},{4,5},{5,6},{6,7},{7,8},{8,9},{9,10},{10,1... | collective-permute-start | bytes 1572872 | tf_op jit(solution)/shard_map/while/body/eval_jaxpr/ppermute | solution.py:18
  110.6 2.1 copy-start.2
  118.3 12.2 %collective-permute-start = (bf16[8,128,256]{2,1,0:T(8,128)(2,1)S(1)}, bf16[8,128,256]{2,1,0:T(8,128)(2,1)S(1)}, u32[]{:S(2)}, u32[]{:S(2)}) collective-permute-start(bf16[8,128,256]{2,1,0:T(8,128)(2,1)S(1)} %get-tuple-element.721), channel_id=1, source_target_pairs={{0,1},{1,2},{2,3},{3,4},{4,5},{5,6},{6,7},{7,8},{8,9},{9,10},{10,1... | collective-permute-start | bytes 1572872 | tf_op jit(solution)/shard_map/while/body/eval_jaxpr/ppermute | solution.py:18
  131.2 2.1 copy-start.2
  138.9 12.2 %collective-permute-start = (bf16[8,128,256]{2,1,0:T(8,128)(2,1)S(1)}, bf16[8,128,256]{2,1,0:T(8,128)(2,1)S(1)}, u32[]{:S(2)}, u32[]{:S(2)}) collective-permute-start(bf16[8,128,256]{2,1,0:T(8,128)(2,1)S(1)} %get-tuple-element.721), channel_id=1, source_target_pairs={{0,1},{1,2},{2,3},{3,4},{4,5},{5,6},{6,7},{7,8},{8,9},{9,10},{10,1... | collective-permute-start | bytes 1572872 | tf_op jit(solution)/shard_map/while/body/eval_jaxpr/ppermute | solution.py:18
  159.4 12.2 %collective-permute-start = (bf16[8,128,256]{2,1,0:T(8,128)(2,1)S(1)}, bf16[8,128,256]{2,1,0:T(8,128)(2,1)S(1)}, u32[]{:S(2)}, u32[]{:S(2)}) collective-permute-start(bf16[8,128,256]{2,1,0:T(8,128)(2,1)S(1)} %get-tuple-element.721), channel_id=1, source_target_pairs={{0,1},{1,2},{2,3},{3,4},{4,5},{5,6},{6,7},{7,8},{8,9},{9,10},{10,1... | collective-permute-start | bytes 1572872 | tf_op jit(solution)/shard_map/while/body/eval_jaxpr/ppermute | solution.py:18
  180.0 12.2 %collective-permute-start = (bf16[8,128,256]{2,1,0:T(8,128)(2,1)S(1)}, bf16[8,128,256]{2,1,0:T(8,128)(2,1)S(1)}, u32[]{:S(2)}, u32[]{:S(2)}) collective-permute-start(bf16[8,128,256]{2,1,0:T(8,128)(2,1)S(1)} %get-tuple-element.721), channel_id=1, source_target_pairs={{0,1},{1,2},{2,3},{3,4},{4,5},{5,6},{6,7},{7,8},{8,9},{9,10},{10,1... | collective-permute-start | bytes 1572872 | tf_op jit(solution)/shard_map/while/body/eval_jaxpr/ppermute | solution.py:18
  192.9 2.1 copy-start.2
  200.6 12.2 %collective-permute-start = (bf16[8,128,256]{2,1,0:T(8,128)(2,1)S(1)}, bf16[8,128,256]{2,1,0:T(8,128)(2,1)S(1)}, u32[]{:S(2)}, u32[]{:S(2)}) collective-permute-start(bf16[8,128,256]{2,1,0:T(8,128)(2,1)S(1)} %get-tuple-element.721), channel_id=1, source_target_pairs={{0,1},{1,2},{2,3},{3,4},{4,5},{5,6},{6,7},{7,8},{8,9},{9,10},{10,1... | collective-permute-start | bytes 1572872 | tf_op jit(solution)/shard_map/while/body/eval_jaxpr/ppermute | solution.py:18
  213.5 2.1 copy-start.2
  221.2 12.2 %collective-permute-start = (bf16[8,128,256]{2,1,0:T(8,128)(2,1)S(1)}, bf16[8,128,256]{2,1,0:T(8,128)(2,1)S(1)}, u32[]{:S(2)}, u32[]{:S(2)}) collective-permute-start(bf16[8,128,256]{2,1,0:T(8,128)(2,1)S(1)} %get-tuple-element.721), channel_id=1, source_target_pairs={{0,1},{1,2},{2,3},{3,4},{4,5},{5,6},{6,7},{7,8},{8,9},{9,10},{10,1... | collective-permute-start | bytes 1572872 | tf_op jit(solution)/shard_map/while/body/eval_jaxpr/ppermute | solution.py:18
  234.1 2.1 copy-start.2
  241.7 12.2 %collective-permute-start = (bf16[8,128,256]{2,1,0:T(8,128)(2,1)S(1)}, bf16[8,128,256]{2,1,0:T(8,128)(2,1)S(1)}, u32[]{:S(2)}, u32[]{:S(2)}) collective-permute-start(bf16[8,128,256]{2,1,0:T(8,128)(2,1)S(1)} %get-tuple-element.721), channel_id=1, source_target_pairs={{0,1},{1,2},{2,3},{3,4},{4,5},{5,6},{6,7},{7,8},{8,9},{9,10},{10,1... | collective-permute-start | bytes 1572872 | tf_op jit(solution)/shard_map/while/body/eval_jaxpr/ppermute | solution.py:18
  262.3 12.2 %collective-permute-start = (bf16[8,128,256]{2,1,0:T(8,128)(2,1)S(1)}, bf16[8,128,256]{2,1,0:T(8,128)(2,1)S(1)}, u32[]{:S(2)}, u32[]{:S(2)}) collective-permute-start(bf16[8,128,256]{2,1,0:T(8,128)(2,1)S(1)} %get-tuple-element.721), channel_id=1, source_target_pairs={{0,1},{1,2},{2,3},{3,4},{4,5},{5,6},{6,7},{7,8},{8,9},{9,10},{10,1... | collective-permute-start | bytes 1572872 | tf_op jit(solution)/shard_map/while/body/eval_jaxpr/ppermute | solution.py:18
  282.9 12.2 %collective-permute-start = (bf16[8,128,256]{2,1,0:T(8,128)(2,1)S(1)}, bf16[8,128,256]{2,1,0:T(8,128)(2,1)S(1)}, u32[]{:S(2)}, u32[]{:S(2)}) collective-permute-start(bf16[8,128,256]{2,1,0:T(8,128)(2,1)S(1)} %get-tuple-element.721), channel_id=1, source_target_pairs={{0,1},{1,2},{2,3},{3,4},{4,5},{5,6},{6,7},{7,8},{8,9},{9,10},{10,1... | collective-permute-start | bytes 1572872 | tf_op jit(solution)/shard_map/while/body/eval_jaxpr/ppermute | solution.py:18
  295.8 2.1 copy-start.2
  303.4 12.2 %collective-permute-start = (bf16[8,128,256]{2,1,0:T(8,128)(2,1)S(1)}, bf16[8,128,256]{2,1,0:T(8,128)(2,1)S(1)}, u32[]{:S(2)}, u32[]{:S(2)}) collective-permute-start(bf16[8,128,256]{2,1,0:T(8,128)(2,1)S(1)} %get-tuple-element.721), channel_id=1, source_target_pairs={{0,1},{1,2},{2,3},{3,4},{4,5},{5,6},{6,7},{7,8},{8,9},{9,10},{10,1... | collective-permute-start | bytes 1572872 | tf_op jit(solution)/shard_map/while/body/eval_jaxpr/ppermute | solution.py:18
  324.0 12.2 %collective-permute-start = (bf16[8,128,256]{2,1,0:T(8,128)(2,1)S(1)}, bf16[8,128,256]{2,1,0:T(8,128)(2,1)S(1)}, u32[]{:S(2)}, u32[]{:S(2)}) collective-permute-start(bf16[8,128,256]{2,1,0:T(8,128)(2,1)S(1)} %get-tuple-element.721), channel_id=1, source_target_pairs={{0,1},{1,2},{2,3},{3,4},{4,5},{5,6},{6,7},{7,8},{8,9},{9,10},{10,1... | collective-permute-start | bytes 1572872 | tf_op jit(solution)/shard_map/while/body/eval_jaxpr/ppermute | solution.py:18
  344.6 12.2 %collective-permute-start = (bf16[8,128,256]{2,1,0:T(8,128)(2,1)S(1)}, bf16[8,128,256]{2,1,0:T(8,128)(2,1)S(1)}, u32[]{:S(2)}, u32[]{:S(2)}) collective-permute-start(bf16[8,128,256]{2,1,0:T(8,128)(2,1)S(1)} %get-tuple-element.721), channel_id=1, source_target_pairs={{0,1},{1,2},{2,3},{3,4},{4,5},{5,6},{6,7},{7,8},{8,9},{9,10},{10,1... | collective-permute-start | bytes 1572872 | tf_op jit(solution)/shard_map/while/body/eval_jaxpr/ppermute | solution.py:18
  377.1 36.4 %all-to-all-start.1 = ((bf16[8,4,128,256]{3,2,1,0:T(8,128)(2,1)}), bf16[8,4,128,256]{3,2,1,0:T(8,128)(2,1)S(1)}, u32[]{:S(2)}, u32[]{:S(2)}) async-start(bf16[8,4,128,256]{3,2,1,0:T(8,128)(2,1)} %copy.60), calls=%async_computation.1 | async-start | bytes 4194304 | tf_op jit(solution)/shard_map/all_to_all | solution.py:137
  380.8 656.6 %all-gather.3.cloned.1.call-start = ((), (), s32[]{:S(2)}) async-start(), calls=%async_computation.2 | async-start | bytes 33816576 | tf_op jit(solution)/shard_map/all_gather | solution.py:10
  417.4 366.3 %copy-start.10 = (s32[1,1,16]{2,1,0:T(1,128)S(1)}, s32[1,1,16]{2,1,0:T(1,128)}, u32[]{:S(2)}) copy-start(s32[1,1,16]{2,1,0:T(1,128)} %param.27) | copy-start | bytes 196
  417.6 13.4 %collective-permute-start.1 = (f32[8,128,256]{2,0,1:T(8,128)}, f32[8,128,256]{2,0,1:T(8,128)}, u32[]{:S(2)}, u32[]{:S(2)}) collective-permute-start(f32[8,128,256]{2,0,1:T(8,128)} %get-tuple-element.757), channel_id=1, source_target_pairs={{0,1},{1,2},{2,3},{3,4},{4,5},{5,6},{6,7},{7,8},{8,9},{9,10},{10,1... | collective-permute-start | bytes 3145736 | tf_op jit(solution)/shard_map/while/body/eval_jaxpr/ppermute | solution.py:18
  437.6 18.1 %collective-permute-start.1 = (f32[8,128,256]{2,0,1:T(8,128)}, f32[8,128,256]{2,0,1:T(8,128)}, u32[]{:S(2)}, u32[]{:S(2)}) collective-permute-start(f32[8,128,256]{2,0,1:T(8,128)} %get-tuple-element.757), channel_id=1, source_target_pairs={{0,1},{1,2},{2,3},{3,4},{4,5},{5,6},{6,7},{7,8},{8,9},{9,10},{10,1... | collective-permute-start | bytes 3145736 | tf_op jit(solution)/shard_map/while/body/eval_jaxpr/ppermute | solution.py:18
  462.3 18.2 %collective-permute-start.1 = (f32[8,128,256]{2,0,1:T(8,128)}, f32[8,128,256]{2,0,1:T(8,128)}, u32[]{:S(2)}, u32[]{:S(2)}) collective-permute-start(f32[8,128,256]{2,0,1:T(8,128)} %get-tuple-element.757), channel_id=1, source_target_pairs={{0,1},{1,2},{2,3},{3,4},{4,5},{5,6},{6,7},{7,8},{8,9},{9,10},{10,1... | collective-permute-start | bytes 3145736 | tf_op jit(solution)/shard_map/while/body/eval_jaxpr/ppermute | solution.py:18
  487.0 18.2 %collective-permute-start.1 = (f32[8,128,256]{2,0,1:T(8,128)}, f32[8,128,256]{2,0,1:T(8,128)}, u32[]{:S(2)}, u32[]{:S(2)}) collective-permute-start(f32[8,128,256]{2,0,1:T(8,128)} %get-tuple-element.757), channel_id=1, source_target_pairs={{0,1},{1,2},{2,3},{3,4},{4,5},{5,6},{6,7},{7,8},{8,9},{9,10},{10,1... | collective-permute-start | bytes 3145736 | tf_op jit(solution)/shard_map/while/body/eval_jaxpr/ppermute | solution.py:18
  511.7 18.2 %collective-permute-start.1 = (f32[8,128,256]{2,0,1:T(8,128)}, f32[8,128,256]{2,0,1:T(8,128)}, u32[]{:S(2)}, u32[]{:S(2)}) collective-permute-start(f32[8,128,256]{2,0,1:T(8,128)} %get-tuple-element.757), channel_id=1, source_target_pairs={{0,1},{1,2},{2,3},{3,4},{4,5},{5,6},{6,7},{7,8},{8,9},{9,10},{10,1... | collective-permute-start | bytes 3145736 | tf_op jit(solution)/shard_map/while/body/eval_jaxpr/ppermute | solution.py:18
  536.4 18.2 %collective-permute-start.1 = (f32[8,128,256]{2,0,1:T(8,128)}, f32[8,128,256]{2,0,1:T(8,128)}, u32[]{:S(2)}, u32[]{:S(2)}) collective-permute-start(f32[8,128,256]{2,0,1:T(8,128)} %get-tuple-element.757), channel_id=1, source_target_pairs={{0,1},{1,2},{2,3},{3,4},{4,5},{5,6},{6,7},{7,8},{8,9},{9,10},{10,1... | collective-permute-start | bytes 3145736 | tf_op jit(solution)/shard_map/while/body/eval_jaxpr/ppermute | solution.py:18
  561.2 18.2 %collective-permute-start.1 = (f32[8,128,256]{2,0,1:T(8,128)}, f32[8,128,256]{2,0,1:T(8,128)}, u32[]{:S(2)}, u32[]{:S(2)}) collective-permute-start(f32[8,128,256]{2,0,1:T(8,128)} %get-tuple-element.757), channel_id=1, source_target_pairs={{0,1},{1,2},{2,3},{3,4},{4,5},{5,6},{6,7},{7,8},{8,9},{9,10},{10,1... | collective-permute-start | bytes 3145736 | tf_op jit(solution)/shard_map/while/body/eval_jaxpr/ppermute | solution.py:18
  585.9 18.2 %collective-permute-start.1 = (f32[8,128,256]{2,0,1:T(8,128)}, f32[8,128,256]{2,0,1:T(8,128)}, u32[]{:S(2)}, u32[]{:S(2)}) collective-permute-start(f32[8,128,256]{2,0,1:T(8,128)} %get-tuple-element.757), channel_id=1, source_target_pairs={{0,1},{1,2},{2,3},{3,4},{4,5},{5,6},{6,7},{7,8},{8,9},{9,10},{10,1... | collective-permute-start | bytes 3145736 | tf_op jit(solution)/shard_map/while/body/eval_jaxpr/ppermute | solution.py:18
  610.6 18.2 %collective-permute-start.1 = (f32[8,128,256]{2,0,1:T(8,128)}, f32[8,128,256]{2,0,1:T(8,128)}, u32[]{:S(2)}, u32[]{:S(2)}) collective-permute-start(f32[8,128,256]{2,0,1:T(8,128)} %get-tuple-element.757), channel_id=1, source_target_pairs={{0,1},{1,2},{2,3},{3,4},{4,5},{5,6},{6,7},{7,8},{8,9},{9,10},{10,1... | collective-permute-start | bytes 3145736 | tf_op jit(solution)/shard_map/while/body/eval_jaxpr/ppermute | solution.py:18
  635.3 18.2 %collective-permute-start.1 = (f32[8,128,256]{2,0,1:T(8,128)}, f32[8,128,256]{2,0,1:T(8,128)}, u32[]{:S(2)}, u32[]{:S(2)}) collective-permute-start(f32[8,128,256]{2,0,1:T(8,128)} %get-tuple-element.757), channel_id=1, source_target_pairs={{0,1},{1,2},{2,3},{3,4},{4,5},{5,6},{6,7},{7,8},{8,9},{9,10},{10,1... | collective-permute-start | bytes 3145736 | tf_op jit(solution)/shard_map/while/body/eval_jaxpr/ppermute | solution.py:18
  660.1 18.2 %collective-permute-start.1 = (f32[8,128,256]{2,0,1:T(8,128)}, f32[8,128,256]{2,0,1:T(8,128)}, u32[]{:S(2)}, u32[]{:S(2)}) collective-permute-start(f32[8,128,256]{2,0,1:T(8,128)} %get-tuple-element.757), channel_id=1, source_target_pairs={{0,1},{1,2},{2,3},{3,4},{4,5},{5,6},{6,7},{7,8},{8,9},{9,10},{10,1... | collective-permute-start | bytes 3145736 | tf_op jit(solution)/shard_map/while/body/eval_jaxpr/ppermute | solution.py:18
  684.8 18.2 %collective-permute-start.1 = (f32[8,128,256]{2,0,1:T(8,128)}, f32[8,128,256]{2,0,1:T(8,128)}, u32[]{:S(2)}, u32[]{:S(2)}) collective-permute-start(f32[8,128,256]{2,0,1:T(8,128)} %get-tuple-element.757), channel_id=1, source_target_pairs={{0,1},{1,2},{2,3},{3,4},{4,5},{5,6},{6,7},{7,8},{8,9},{9,10},{10,1... | collective-permute-start | bytes 3145736 | tf_op jit(solution)/shard_map/while/body/eval_jaxpr/ppermute | solution.py:18
  709.5 18.2 %collective-permute-start.1 = (f32[8,128,256]{2,0,1:T(8,128)}, f32[8,128,256]{2,0,1:T(8,128)}, u32[]{:S(2)}, u32[]{:S(2)}) collective-permute-start(f32[8,128,256]{2,0,1:T(8,128)} %get-tuple-element.757), channel_id=1, source_target_pairs={{0,1},{1,2},{2,3},{3,4},{4,5},{5,6},{6,7},{7,8},{8,9},{9,10},{10,1... | collective-permute-start | bytes 3145736 | tf_op jit(solution)/shard_map/while/body/eval_jaxpr/ppermute | solution.py:18
  734.2 18.2 %collective-permute-start.1 = (f32[8,128,256]{2,0,1:T(8,128)}, f32[8,128,256]{2,0,1:T(8,128)}, u32[]{:S(2)}, u32[]{:S(2)}) collective-permute-start(f32[8,128,256]{2,0,1:T(8,128)} %get-tuple-element.757), channel_id=1, source_target_pairs={{0,1},{1,2},{2,3},{3,4},{4,5},{5,6},{6,7},{7,8},{8,9},{9,10},{10,1... | collective-permute-start | bytes 3145736 | tf_op jit(solution)/shard_map/while/body/eval_jaxpr/ppermute | solution.py:18
  759.0 18.2 %collective-permute-start.1 = (f32[8,128,256]{2,0,1:T(8,128)}, f32[8,128,256]{2,0,1:T(8,128)}, u32[]{:S(2)}, u32[]{:S(2)}) collective-permute-start(f32[8,128,256]{2,0,1:T(8,128)} %get-tuple-element.757), channel_id=1, source_target_pairs={{0,1},{1,2},{2,3},{3,4},{4,5},{5,6},{6,7},{7,8},{8,9},{9,10},{10,1... | collective-permute-start | bytes 3145736 | tf_op jit(solution)/shard_map/while/body/eval_jaxpr/ppermute | solution.py:18
  783.7 2.9 copy-start.4
  1057.0 5.0 copy-start.1
  (25 other events, 35.0 us)
Sparse Core Ops, SparseCore 0:
  787.8 249.5 all-gather.2
